TPU v7x, 32 devices: a whole 2x2x4 slice. The times are simulated.
32 devices in a mesh: ens: 2 (over x), gy: 16 (over z, y, core).
Axes of the slice: x: 2, y: 2, z: 4, core: 2. Of those that a mesh axis runs over, the one named last changes fastest.
Arguments:
- forcing: float32 [512, 16384], P(('ens', 'gy')), parts along dimension 0, may hold values from -6 to 6
- east: float32 [256, 16384], P('gy'), may hold values from 0.5 to 2
- north: float32 [256, 16384], P('gy'), may hold values from 0.5 to 2
- storage: float32 [256, 16384], P('gy'), may hold values from 0.05 to 0.5
- coarse_inverse: float32 [64, 16, 16], replicated, as said below
- membership: int32 [4, 256], replicated, may hold values from 0 to 63, as said below
- land: int32 [4, 256], replicated, may hold values 0 or 1
Outputs:
- solution: float32 [512, 16384], P(('ens', 'gy')), parts along dimension 0
- residual: float32 [512, 16384], P(('ens', 'gy')), parts along dimension 0
There are 2 independent parts, one for each index of `ens`. A program takes and returns all parts, laid end to end along the dimension named above; an argument that names none is the same for every part. Nothing has to cross between parts.
Inputs may be any that keep to these rules, and one draw needn't show every extreme that they name: `coarse_inverse`: each inverse is symmetric positive definite. `membership`: every basin holds one tile or more.
All inputs are finite; a program needn't handle non-finite values.
Results may differ from a plain program's by a relative error of at most 0.0003.
Values sent between devices are 32-bit elements; how exact they have to be, the bound alone decides.
A program may use at most 64 MiB of HBM per device.

v0:
```python
import jax
import jax.numpy as jnp
from jax import lax
from jax.sharding import PartitionSpec as P

TILE = 64
ORDER = 4
ITERS = 2


HIGHEST = lax.Precision.HIGHEST


def shifted(block, axis, distance):
    devices = range(lax.axis_size(axis))
    route = [(i - distance, i) for i in devices if i - distance in devices]
    return lax.ppermute(block, axis, route)


def padded_2(shard, sides, width):
    for axis, dim in sides:
        devices, length = (lax.axis_size(axis), shard.shape[dim])
        up = [(i, (i + 1) % devices) for i in range(devices - 1)]
        down = [(j, i) for i, j in up]
        last = lax.slice_in_dim(shard, length - width, length, axis=dim)
        leading = lax.slice_in_dim(shard, 0, width, axis=dim)
        before = lax.ppermute(last, axis, up)
        after = lax.ppermute(leading, axis, down)
        shard = jnp.concatenate([before, shard, after], axis=dim)
    return shard


def body(forcing, east, north, storage, coarse_inverse, membership, land):
    rows, width = forcing.shape
    index = lax.axis_index("gy")
    start = index * rows
    basins = coarse_inverse.shape[0]
    coarse = coarse_inverse.shape[1]
    tile = TILE
    order = ORDER
    tiles_x = width // tile
    tile_rows = membership.shape[0]
    total_rows = tile_rows * tile
    row_ids = start + jnp.arange(rows + 1, dtype=jnp.int32)
    tile_of_row = jnp.minimum(row_ids // tile, tile_rows - 1)
    picker = (tile_of_row[:, None] == jnp.arange(tile_rows, dtype=jnp.int32)[None, :]).astype(
        jnp.float32
    )
    land_rows = jnp.dot(picker, land.astype(jnp.float32), precision=HIGHEST)
    inside = (row_ids < total_rows).astype(jnp.float32)
    wet_rows = jnp.repeat((1.0 - land_rows) * inside[:, None], tile, axis=1)
    wet = wet_rows[:rows]
    above = wet_rows[1:]
    east_face = east * wet * jnp.roll(wet, -1, axis=1)
    north_face = north * wet * above
    lower = shifted(north_face[rows - 1 :], "gy", 1)
    south_face = jnp.concatenate([lower, north_face[:-1]], axis=0)
    west_face = jnp.roll(east_face, 1, axis=1)
    center = 1.0 - wet + wet * storage + east_face + west_face + north_face + south_face
    jacobi = 1.0 / center
    degree = jnp.arange(order).astype(jnp.float32)
    local_rows = (start % tile + jnp.arange(rows, dtype=jnp.int32)).astype(jnp.float32)
    row_modes = jnp.cos(jnp.pi * degree[:, None] * (local_rows[None, :] + 0.5) / tile)
    local_cols = (jnp.arange(width, dtype=jnp.int32) % tile).astype(jnp.float32)
    col_modes = jnp.cos(jnp.pi * degree[:, None] * (local_cols[None, :] + 0.5) / tile)
    my_basins = lax.dynamic_slice_in_dim(membership, start // tile, 1, 0)[0]
    owned = (my_basins[:, None] == jnp.arange(basins, dtype=jnp.int32)[None, :]).astype(jnp.float32)

    def operate(field):
        padded = padded_2(field, (("gy", 0),), 1)
        return (
            center * field
            - east_face * jnp.roll(field, -1, axis=1)
            - west_face * jnp.roll(field, 1, axis=1)
            - north_face * padded[2:]
            - south_face * padded[:-2]
        )

    def moments(field):
        lifted = jnp.dot(row_modes, wet * field, precision=HIGHEST)
        product = (lifted[:, None, :] * col_modes[None, :, :]).reshape(coarse, tiles_x, tile)
        per_tile = jnp.sum(product, axis=2)
        return jnp.dot(per_tile, owned, precision=HIGHEST).T

    def spread(coef):
        per_tile = jnp.dot(owned, coef, precision=HIGHEST)
        per_col = jnp.repeat(per_tile.T, tile, axis=1).reshape(order, order, width)
        lifted = jnp.sum(per_col * col_modes[None, :, :], axis=1)
        return wet * jnp.dot(row_modes.T, lifted, precision=HIGHEST)

    def reduce_coarse(partial_value, dots):
        return lax.psum((partial_value, dots), "gy")

    def expand(held_g):
        held_c = jnp.einsum("nij,nj->ni", coarse_inverse, held_g, precision=HIGHEST)
        return (held_c, jnp.sum(held_g * held_c))

    solution = jnp.zeros_like(forcing)
    residual = forcing
    smoothed = jacobi * residual
    held_g, dots = reduce_coarse(moments(residual), jnp.stack([jnp.sum(residual * smoothed)]))
    full_c, coarse_dot = expand(held_g)
    precond = smoothed + spread(full_c)
    energy = dots[0] + coarse_dot
    direction = precond
    image = operate(precond)
    held_s, dots = reduce_coarse(moments(image), jnp.stack([jnp.sum(image * precond)]))
    alpha = energy / dots[0]
    along = image
    for step in range(ITERS):
        solution = solution + alpha * direction
        residual = residual - alpha * along
        if step + 1 < ITERS:
            held_g = held_g - alpha * held_s
            smoothed = jacobi * residual
            full_c, coarse_dot = expand(held_g)
            precond = smoothed + spread(full_c)
            image = operate(precond)
            held_w, dots = reduce_coarse(
                moments(image), jnp.stack([jnp.sum(residual * smoothed), jnp.sum(image * precond)])
            )
            energy_next = dots[0] + coarse_dot
            beta = energy_next / energy
            alpha = energy_next / (dots[1] - beta * energy_next / alpha)
            direction = precond + beta * direction
            along = image + beta * along
            held_s = held_w + beta * held_s
            energy = energy_next
    return (solution, residual)


def solution(mesh):
    return jax.shard_map(
        body,
        mesh=mesh,
        in_specs=(
            P(("ens", "gy"), None),
            P("gy", None),
            P("gy", None),
            P("gy", None),
            P(),
            P(),
            P(),
        ),
        out_specs=(P(("ens", "gy"), None), P(("ens", "gy"), None)),
        check_vma=False,
    )
```

profile of v0, /device:TPU:0, one launch (start us, length us, event | category | flops | bytes accessed | tf_op | source)
XLA Modules:
  0.0 178.8 jit_solution(6533411401946666361)
XLA Ops:
  0.6 0.0 copy-start
  0.7 0.9 fusion.2
  1.6 0.6 broadcast_in_dim.8
  2.2 0.7 slice.95
  2.9 1.3 slice.123
  4.2 0.6 broadcast_in_dim.9
  4.8 1.6 slice.101
  6.4 2.6 %maximum_multiply_fusion = (f32[16,16384]{1,0:T(8,128)S(1)}, f32[16,16384]{1,0:T(8,128)S(1)}) fusion(f32[16,1]{1,0:T(8,128)S(1)} %slice.124, f32[16,16383]{1,0:T(8,128)} %slice.123, f32[16,16384]{1,0:T(8,128)} %param.8, f32[16,16384]{1,0:T(8,128)S(1)} %slice.95, f32[16,16384]{1,0:T(8,128)} %slice.101, f32[16,16384]{1,0:T(8,128)} %param.9), kind=kLoop, calls=%fused_computation.18 | loop fusion | flops 1310720 | bytes 7340032 | tf_op jit(solution)/shard_map/mul | solution.py:54
  9.0 0.7 slice.128
  9.6 2.4 %collective-permute-start = (f32[1,16384]{1,0:T(1,128)}, f32[1,16384]{1,0:T(1,128)S(1)}, u32[]{:S(2)}, u32[]{:S(2)}) collective-permute-start(f32[1,16384]{1,0:T(1,128)} %slice.128), channel_id=1, source_target_pairs={{0,1},{1,2},{2,3},{3,4},{4,5},{5,6},{6,7},{7,8},{8,9},{9,10},{10,1... | collective-permute-start | bytes 196616 | tf_op jit(solution)/shard_map/ppermute | solution.py:17
  12.1 1.9 %multiply_cosine_fusion = f32[4,16384]{1,0:T(4,128)S(1)} fusion(f32[16384]{0:T(1024)S(1)} %fusion.24, f32[4]{0:T(128)S(1)} %convert_multiply_fusion), kind=kLoop, calls=%fused_computation.47 | loop fusion | flops 131072 | bytes 327696 | tf_op jit(solution)/shard_map/cos | solution.py:65
  14.0 2.0 %fusion.17 = f32[4,16384]{1,0:T(4,128)S(1)} fusion(f32[16,16384]{1,0:T(8,128)S(1)} %slice.95, f32[16,16384]{1,0:T(8,128)} %param.7, f32[16]{0:T(128)S(1)} %convert_add_fusion, f32[4]{0:T(128)S(1)} %convert_multiply_fusion), kind=kOutput, calls=%fused_computation.39 | convolution fusion | flops 12845184 | bytes 2359376 | tf_op jit(solution)/shard_map/dot_general | solution.py:80
  16.0 1.2 broadcast_multiply_fusion.1
  17.2 3.2 %mul.267 = f32[16,256,64]{2,1,0:T(8,128)} reshape(f32[4,4,16384]{2,1,0:T(4,128)} %broadcast_multiply_fusion.1) | data formatting | bytes 2097152 | tf_op jit(solution)/shard_map/mul | solution.py:81
  20.4 2.2 %reduce_sum.91 = f32[16,256]{1,0:T(8,128)S(1)} reduce(f32[16,256,64]{2,1,0:T(8,128)} %mul.267, f32[]{:T(128)} %constant.66.clone.1), dimensions={2}, to_apply=%region_2.3 | reduce | flops 258048 | bytes 1064964 | tf_op jit(solution)/shard_map/reduce_sum | solution.py:82
  22.6 0.2 fusion.22
  22.9 34.4 %psum.36 = f32[64,16]{0,1:T(8,128)S(1)} all-reduce(f32[64,16]{0,1:T(8,128)S(1)} %fusion.22), channel_id=1, replica_groups=mesh['ens'=2,'gy'=16] {'gy'}, use_global_device_ids=true, to_apply=%region_3.4 | all-reduce | flops 1024 | bytes 8192 | tf_op jit(solution)/shard_map/psum | solution.py:92
  57.2 0.9 multiply_reduce_fusion.7
  58.2 0.2 fusion.21
  58.4 0.1 slice.125
  58.5 2.0 %broadcast_in_dim.10 = f32[16,256,64]{2,1,0:T(8,128)} broadcast(f32[16,256]{1,0:T(8,128)S(1)} %fusion.21), dimensions={0,1} | broadcast | bytes 1064960 | tf_op jit(solution)/shard_map/broadcast_in_dim | solution.py:87
  60.5 3.0 %reshape_reshape.6 = f32[4,4,16384]{2,1,0:T(4,128)} reshape(f32[16,256,64]{2,1,0:T(8,128)} %broadcast_in_dim.10) | data formatting | bytes 2097152 | tf_op jit(solution)/shard_map/reshape;reshape | solution.py:87
  63.5 2.1 %multiply_reduce_fusion.4 = f32[4,16384]{1,0:T(4,128)S(1)} fusion(f32[4,4,16384]{2,1,0:T(4,128)} %reshape_reshape.6, f32[4,16384]{1,0:T(4,128)S(1)} %multiply_cosine_fusion), kind=kLoop, calls=%fused_computation.38 | loop fusion | flops 458752 | bytes 1572864 | tf_op jit(solution)/shard_map/reduce_sum | solution.py:88
  65.5 0.6 multiply_reduce_fusion.9
  66.2 0.0 collective-permute-done
  66.2 2.5 %multiply_reduce_fusion.5 = (f32[]{:T(128)}, f32[16,16384]{1,0:T(8,128)S(1)}) fusion(f32[16,16384]{1,0:T(8,128)S(1)} %copy-done.1, f32[15,16384]{1,0:T(8,128)S(1)} %bitcast.17, f32[1,16384]{1,0:T(1,128)S(1)} %collective-permute-done, f32[16,16384]{1,0:T(8,128)S(1)} %get-tuple-element.25, f32[16,16383]{1,0:T(8,128)S(1)} %bitcast.20, f32[16,1]{1,0:T(8,128)S(1)} %slice.125, ...), kind=kLoop, calls=%fused_computation.41 | loop fusion | flops 3407871 | bytes 8388612 | tf_op jit(solution)/shard_map/reduce_sum | solution.py:101
  68.7 1.4 fusion.1
  70.1 0.1 fusion.58
  70.2 0.3 fusion.56
  70.5 1.3 collective-permute-start.1
  71.8 3.2 %collective-permute-start.2 = (f32[1,16384]{1,0:T(1,128)S(1)}, f32[1,16384]{1,0:T(1,128)S(1)}, u32[]{:S(2)}, u32[]{:S(2)}) collective-permute-start(f32[1,16384]{1,0:T(1,128)S(1)} %get-tuple-element.23), channel_id=1, source_target_pairs={{0,1},{1,2},{2,3},{3,4},{4,5},{5,6},{6,7},{7,8},{8,9},{9,10},{10,1... | collective-permute-start | bytes 196616 | tf_op jit(solution)/shard_map/ppermute | solution.py:27
  75.1 0.1 fusion.57
  75.1 0.0 collective-permute-done.1
  75.1 0.6 collective-permute-done.2
  75.8 0.0 copy-done.4
  75.8 1.6 multiply_reduce_fusion.3
  77.4 1.0 copy-done.8
  78.3 0.7 fusion.15
  79.1 1.2 broadcast_multiply_fusion
  80.2 3.2 %mul.286 = f32[16,256,64]{2,1,0:T(8,128)} reshape(f32[4,4,16384]{2,1,0:T(4,128)} %broadcast_multiply_fusion) | data formatting | bytes 2097152 | tf_op jit(solution)/shard_map/mul | solution.py:81
  83.5 2.2 %reduce_sum.96 = f32[16,256]{1,0:T(8,128)S(1)} reduce(f32[16,256,64]{2,1,0:T(8,128)} %mul.286, f32[]{:T(128)} %constant.66.clone.1), dimensions={2}, to_apply=%region_9.10 | reduce | flops 258048 | bytes 1064964 | tf_op jit(solution)/shard_map/reduce_sum | solution.py:82
  85.7 0.2 fusion.20
  85.9 31.4 %all-reduce = (f32[64,16]{0,1:T(8,128)S(1)}, f32[]{:T(128)}, f32[]{:T(128)}) all-reduce(f32[64,16]{0,1:T(8,128)S(1)} %fusion.20, f32[]{:T(128)} %get-tuple-element.9, f32[]{:T(128)} %get-tuple-element.7), channel_id=1, replica_groups=mesh['ens'=2,'gy'=16] {'gy'}, use_global_device_ids=true, to_apply=%region_10.11 | all-reduce | flops 1026 | bytes 8208 | tf_op jit(solution)/shard_map/psum | solution.py:92
  119.3 0.9 multiply_reduce_fusion.6
  120.2 0.2 fusion.19
  120.4 2.0 %broadcast_in_dim.11 = f32[16,256,64]{2,1,0:T(8,128)} broadcast(f32[16,256]{1,0:T(8,128)S(1)} %fusion.19), dimensions={0,1} | broadcast | bytes 1064960 | tf_op jit(solution)/shard_map/broadcast_in_dim | solution.py:87
  122.4 3.0 %reshape_reshape.7 = f32[4,4,16384]{2,1,0:T(4,128)} reshape(f32[16,256,64]{2,1,0:T(8,128)} %broadcast_in_dim.11) | data formatting | bytes 2097152 | tf_op jit(solution)/shard_map/reshape;reshape | solution.py:87
  125.5 2.1 %multiply_reduce_fusion.1 = f32[4,16384]{1,0:T(4,128)S(1)} fusion(f32[4,4,16384]{2,1,0:T(4,128)} %reshape_reshape.7, f32[4,16384]{1,0:T(4,128)S(1)} %multiply_cosine_fusion), kind=kLoop, calls=%fused_computation.32 | loop fusion | flops 458752 | bytes 1572864 | tf_op jit(solution)/shard_map/reduce_sum | solution.py:88
  127.5 3.0 %fusion = f32[16,16384]{1,0:T(8,128)S(1)} fusion(f32[16,16384]{1,0:T(8,128)S(1)} %slice.95, f32[4,16384]{1,0:T(4,128)S(1)} %multiply_reduce_fusion.1, f32[16,16384]{1,0:T(8,128)S(1)} %copy-done.2, f32[16,16384]{1,0:T(8,128)} %copy-done.8, f32[]{:T(128)S(6)} %div.65, f32[16]{0:T(128)S(1)} %convert_add_fusion, f32[4]{0:T(128)S(1)} %convert_multiply_fusion, ...), kind=kOutput, calls=%fused_computation.1 | convolution fusion | flops 14155904 | bytes 5505108 | tf_op jit(solution)/shard_map/dot_general | solution.py:89
  130.5 0.0 copy-start.5
  130.5 0.1 fusion.55
  130.6 0.0 copy-start.9
  130.6 0.3 fusion.53
  131.0 1.4 collective-permute-start.3
  132.4 3.0 %collective-permute-start.4 = (f32[1,16384]{1,0:T(1,128)S(1)}, f32[1,16384]{1,0:T(1,128)S(1)}, u32[]{:S(2)}, u32[]{:S(2)}) collective-permute-start(f32[1,16384]{1,0:T(1,128)S(1)} %get-tuple-element.17), channel_id=1, source_target_pairs={{0,1},{1,2},{2,3},{3,4},{4,5},{5,6},{6,7},{7,8},{8,9},{9,10},{10,1... | collective-permute-start | bytes 196616 | tf_op jit(solution)/shard_map/ppermute | solution.py:27
  135.4 0.1 fusion.54
  135.5 0.0 collective-permute-done.3
  135.5 0.8 collective-permute-done.4
  136.3 2.7 %multiply_reduce_fusion = (f32[]{:T(128)}, f32[16,16384]{1,0:T(8,128)}, f32[]{:T(128)}) fusion(f32[16,16384]{1,0:T(8,128)S(1)} %fusion, f32[1,16384]{1,0:T(1,128)S(1)} %collective-permute-done.4, f32[15,16384]{1,0:T(8,128)S(1)} %bitcast.19, f32[1,16384]{1,0:T(1,128)S(1)} %collective-permute-done, f32[16,16384]{1,0:T(8,128)S(1)} %get-tuple-element.25, ...), kind=kLoop, calls=%fused_computation.31 | loop fusion | flops 6029310 | bytes 11665420 | tf_op jit(solution)/shard_map/reduce_sum | solution.py:120
  139.0 1.3 pad_maximum_fusion.6
  140.4 0.6 multiply_reduce_fusion.8
  141.0 30.5 %psum.39 = f32[2]{0:T(128)S(1)} all-reduce(f32[2]{0:T(128)S(1)} %pad_maximum_fusion.6), channel_id=1, replica_groups=mesh['ens'=2,'gy'=16] {'gy'}, use_global_device_ids=true, to_apply=%region_13.14 | all-reduce | flops 2 | bytes 16 | tf_op jit(solution)/shard_map/psum | solution.py:92
  171.5 0.7 fusion.60
  174.8 4.0 %multiply_subtract_fusion = (f32[16,16384]{1,0:T(8,128)}, f32[16,16384]{1,0:T(8,128)}) fusion(f32[16,16384]{1,0:T(8,128)} %get-tuple-element.6, f32[16,16384]{1,0:T(8,128)} %copy-done.8, f32[]{:T(128)S(6)} %div.66, f32[]{:T(128)S(6)} %div.68, f32[16,16384]{1,0:T(8,128)S(1)} %copy-done.3, f32[]{:T(128)S(6)} %div.65, f32[16,16384]{1,0:T(8,128)} %copy-done.5, ...), kind=kLoop, calls=%fused_computation.29 | loop fusion | flops 2883584 | bytes 7340044 | tf_op jit(solution)/shard_map/sub | solution.py:112
  (24 shorter events, 0.1 us)
Async XLA Ops:
  0.6 19.8 %copy-start = (s32[4,256]{1,0:T(4,128)S(1)}, s32[4,256]{1,0:T(4,128)}, u32[]{:S(2)}) copy-start(s32[4,256]{1,0:T(4,128)} %param.12) | copy-start | bytes 12292
  9.6 56.5 %collective-permute-start = (f32[1,16384]{1,0:T(1,128)}, f32[1,16384]{1,0:T(1,128)S(1)}, u32[]{:S(2)}, u32[]{:S(2)}) collective-permute-start(f32[1,16384]{1,0:T(1,128)} %slice.128), channel_id=1, source_target_pairs={{0,1},{1,2},{2,3},{3,4},{4,5},{5,6},{6,7},{7,8},{8,9},{9,10},{10,1... | collective-permute-start | bytes 196616 | tf_op jit(solution)/shard_map/ppermute | solution.py:17
  63.5 2.7 %copy-start.1 = (f32[16,16384]{1,0:T(8,128)S(1)}, f32[16,16384]{1,0:T(8,128)}, u32[]{:S(2)}) copy-start(f32[16,16384]{1,0:T(8,128)} %param.7) | copy-start | bytes 3145732
  68.7 7.1 %copy-start.6 = (f32[16,16384]{1,0:T(8,128)}, f32[16,16384]{1,0:T(8,128)S(1)}, u32[]{:S(2)}) copy-start(f32[16,16384]{1,0:T(8,128)S(1)} %get-tuple-element.10) | copy-start | bytes 3145732
  70.1 5.7 %copy-start.4 = (f32[16,16384]{1,0:T(8,128)}, f32[16,16384]{1,0:T(8,128)S(1)}, u32[]{:S(2)}) copy-start(f32[16,16384]{1,0:T(8,128)S(1)} %fusion.1) | copy-start | bytes 3145732
  70.5 4.6 %collective-permute-start.1 = (f32[1,16384]{1,0:T(1,128)S(1)}, f32[1,16384]{1,0:T(1,128)S(1)}, u32[]{:S(2)}, u32[]{:S(2)}) collective-permute-start(f32[1,16384]{1,0:T(1,128)S(1)} %get-tuple-element.22), channel_id=1, source_target_pairs={{1,0},{2,1},{3,2},{4,3},{5,4},{6,5},{7,6},{8,7},{9,8},{10,9},{11,1... | collective-permute-start | bytes 196616 | tf_op jit(solution)/shard_map/ppermute | solution.py:28
  71.8 3.9 %collective-permute-start.2 = (f32[1,16384]{1,0:T(1,128)S(1)}, f32[1,16384]{1,0:T(1,128)S(1)}, u32[]{:S(2)}, u32[]{:S(2)}) collective-permute-start(f32[1,16384]{1,0:T(1,128)S(1)} %get-tuple-element.23), channel_id=1, source_target_pairs={{0,1},{1,2},{2,3},{3,4},{4,5},{5,6},{6,7},{7,8},{8,9},{9,10},{10,1... | collective-permute-start | bytes 196616 | tf_op jit(solution)/shard_map/ppermute | solution.py:27
  77.4 1.0 copy-start.8
  125.5 2.1 %copy-start.2 = (f32[16,16384]{1,0:T(8,128)S(1)}, f32[16,16384]{1,0:T(8,128)}, u32[]{:S(2)}) copy-start(f32[16,16384]{1,0:T(8,128)} %param.7) | copy-start | bytes 3145732
  130.5 5.8 %copy-start.5 = (f32[16,16384]{1,0:T(8,128)}, f32[16,16384]{1,0:T(8,128)S(1)}, u32[]{:S(2)}) copy-start(f32[16,16384]{1,0:T(8,128)S(1)} %fusion) | copy-start | bytes 3145732
  130.6 5.7 %copy-start.7 = (f32[16,16384]{1,0:T(8,128)S(1)}, f32[16,16384]{1,0:T(8,128)}, u32[]{:S(2)}) copy-start(f32[16,16384]{1,0:T(8,128)} %copy-done.6) | copy-start | bytes 3145732
  130.6 5.7 %copy-start.9 = (f32[16,16384]{1,0:T(8,128)S(1)}, f32[16,16384]{1,0:T(8,128)}, u32[]{:S(2)}) copy-start(f32[16,16384]{1,0:T(8,128)} %copy-done.8) | copy-start | bytes 3145732
  131.0 4.5 %collective-permute-start.3 = (f32[1,16384]{1,0:T(1,128)S(1)}, f32[1,16384]{1,0:T(1,128)S(1)}, u32[]{:S(2)}, u32[]{:S(2)}) collective-permute-start(f32[1,16384]{1,0:T(1,128)S(1)} %get-tuple-element.16), channel_id=1, source_target_pairs={{1,0},{2,1},{3,2},{4,3},{5,4},{6,5},{7,6},{8,7},{9,8},{10,9},{11,1... | collective-permute-start | bytes 196616 | tf_op jit(solution)/shard_map/ppermute | solution.py:28
  132.4 3.9 %collective-permute-start.4 = (f32[1,16384]{1,0:T(1,128)S(1)}, f32[1,16384]{1,0:T(1,128)S(1)}, u32[]{:S(2)}, u32[]{:S(2)}) collective-permute-start(f32[1,16384]{1,0:T(1,128)S(1)} %get-tuple-element.17), channel_id=1, source_target_pairs={{0,1},{1,2},{2,3},{3,4},{4,5},{5,6},{6,7},{7,8},{8,9},{9,10},{10,1... | collective-permute-start | bytes 196616 | tf_op jit(solution)/shard_map/ppermute | solution.py:27
  136.3 38.5 %copy-start.3 = (f32[16,16384]{1,0:T(8,128)S(1)}, f32[16,16384]{1,0:T(8,128)}, u32[]{:S(2)}) copy-start(f32[16,16384]{1,0:T(8,128)} %param.7) | copy-start | bytes 3145732
where the time goes:
time: 180 us; the launch traced here: 179 us
  blocking collectives  96.3 us (54%)
  other arithmetic  30.6 us (17%)
  local copies, waits for them, and re-layouts  24.8 us (14%)
  starting transfers between devices  11.4 us (6%)
  matrix products  8.81 us (5%)
  between operations  5.5 us (3%)
    psum x3, blocking collectives, reduce_coarse(): return lax.psum((partial_value, dots), 'gy')  96.3 us
    mul x2, local copies, waits for them, and re-layouts, moments(): lifted[:, None, :] * col_modes[None, :, :]  6.46 us
    ppermute x2, starting transfers between devices, padded_2(): before = lax.ppermute(last, axis, up)  6.25 us
    another operation x2, local copies, waits for them, and re-layouts, spread(): per_col = jnp.repeat(per_tile.T, tile, axis=1).reshape(order, order, width)  6.05 us
    reduce_sum x2, other arithmetic, moments(): per_tile = jnp.sum(product, axis=2)  4.4 us
    dot_general x2, matrix products, spread(): return wet * jnp.dot(row_modes.T, lifted, precision=HIGHEST)  4.34 us
    reduce_sum x2, other arithmetic, body(): jnp.sum(image * precond)  4.28 us
    reduce_sum x2, other arithmetic, spread(): lifted = jnp.sum(per_col * col_modes[None, :, :], axis=1)  4.13 us
  transfers between devices with their start and end apart: 5, of which 2 were waited for; matrix products, arithmetic and copies ran while one was open for 11% of the time, Pallas kernels for 0%

commit v1 on v0

v1 whole, which is shorter than its diff:
```python
import functools

import jax
import jax.numpy as jnp
import numpy as np
from jax import lax
from jax.experimental import pallas as pl
from jax.experimental.pallas import tpu as pltpu
from jax.sharding import PartitionSpec as P

TILE = 64
ORDER = 4
LANES = 128
BLOCKS = 8
HIGHEST = lax.Precision.HIGHEST
MESH = pl.DeviceIdType.MESH


def tables():
    degree = np.arange(ORDER, dtype=np.float64)
    local = np.arange(TILE, dtype=np.float64)
    modes = np.cos(np.pi * degree[:, None] * (local[None, :] + 0.5) / TILE).astype(np.float32)
    by_row = np.repeat(modes[:, :, None], LANES, axis=2)
    kron = np.zeros((ORDER * ORDER, ORDER * LANES), np.float32)
    for p in range(ORDER):
        for q in range(ORDER):
            kron[p * ORDER + q, p * LANES : (p + 1) * LANES] = np.tile(modes[q], LANES // TILE)
    return by_row, kron


def dot(a, b, contract=((1,), (0,))):
    return lax.dot_general(
        a, b, (contract, ((), ())), precision=HIGHEST, preferred_element_type=jnp.float32
    )


def kernel(
    n,
    forcing_hbm, east_hbm, north_hbm, storage_hbm, inverse_hbm,
    membership_ref, land_ref, by_row_ref, kron_ref,
    sol_ref, res_ref,
    f_ref, east_ref, north_ref, storage_ref, inv_ref,
    e_ref, w_ref, s_ref, c_ref, j_ref, sm_ref, q_ref, z0_ref, z1_ref, im0_ref, im1_ref,
    mask_ref, own_ref, spread_ref, edge_ref, lift_ref, ct_ref,
    nlo_ref, smlo_ref, smhi_ref, qlo_ref, qhi_ref,
    send_ref, recv_ref,
    in_sem, row_send_sem, row_recv_sem, all_send_sem, all_recv_sem,
):
    rows, width = f_ref.shape
    basins = inv_ref.shape[0]
    coarse = inv_ref.shape[1]
    blocks = width // LANES
    half = LANES // 2
    span = BLOCKS * LANES
    chunks = width // span
    tile_rows = membership_ref.shape[0]
    me = lax.axis_index("gy")
    start = me * rows
    has_up = me < n - 1
    has_down = me > 0

    def load(src, dst, k):
        return pltpu.make_async_copy(src, dst, in_sem.at[k])

    loads = [
        load(forcing_hbm, f_ref, 0),
        load(north_hbm, north_ref, 1),
        load(east_hbm, east_ref.at[:, pl.ds(LANES, width)], 2),
        load(east_hbm.at[:, pl.ds(width - LANES, LANES)], east_ref.at[:, pl.ds(0, LANES)], 3),
        load(storage_hbm, storage_ref, 4),
        load(inverse_hbm, inv_ref, 5),
    ]
    for copy in loads:
        copy.start()

    barrier = pltpu.get_barrier_semaphore()

    def greet(k, carry):
        pl.semaphore_signal(
            barrier, inc=1, device_id={"gy": lax.rem(me + k, n)}, device_id_type=MESH
        )
        return carry

    lax.fori_loop(1, n, greet, 0)

    own_row = start // TILE
    up_row = jnp.minimum((start + rows) // TILE, tile_rows - 1)
    down_row = jnp.maximum(start - 1, 0) // TILE
    local_own = pl.multiple_of(lax.rem(start, TILE), rows)
    local_up = lax.rem(start + rows, TILE)
    local_down = lax.rem(start + TILE - 1, TILE)

    tiles = membership_ref.shape[1]
    tile_id = lax.broadcasted_iota(jnp.int32, (blocks, tiles), 1)
    block_id = lax.broadcasted_iota(jnp.int32, (blocks, tiles), 0)
    even = tile_id == 2 * block_id
    odd = tile_id == 2 * block_id + 1
    lane = lax.broadcasted_iota(jnp.int32, (blocks, LANES), 1)
    left = lane < half
    basin_of_lane = jnp.where(left, lane, lane - half)

    def columns(table, row):
        line = table[pl.ds(row, 1), :].astype(jnp.float32)
        first = jnp.sum(jnp.where(even, line, 0.0), axis=1, keepdims=True)
        second = jnp.sum(jnp.where(odd, line, 0.0), axis=1, keepdims=True)
        return (
            jnp.broadcast_to(first, (blocks, LANES)),
            jnp.broadcast_to(second, (blocks, LANES)),
        )

    def owned(row, wet0, wet1):
        first, second = columns(membership_ref, row)
        which = jnp.where(left, first, second)
        hit = which == basin_of_lane.astype(jnp.float32)
        return jnp.where(hit, jnp.where(left, wet0, wet1), 0.0)

    def wets(row):
        first, second = columns(land_ref, row)
        return 1.0 - first, 1.0 - second

    wet0, wet1 = wets(own_row)
    wet = jnp.where(left, wet0, wet1)
    east_wet = jnp.where(
        lane == half - 1, wet1, jnp.where(lane == LANES - 1, pltpu.roll(wet0, blocks - 1, 0), wet)
    )
    west_wet = jnp.where(lane == 0, pltpu.roll(wet1, 1, 0), jnp.where(lane == half, wet0, wet))
    up0, up1 = wets(up_row)
    down0, down1 = wets(down_row)
    mask_ref[0] = wet
    mask_ref[1] = wet * east_wet
    mask_ref[2] = wet * west_wet
    mask_ref[3] = jnp.where(has_up, wet * jnp.where(left, up0, up1), 0.0)
    mask_ref[4] = jnp.where(has_down, wet * jnp.where(left, down0, down1), 0.0)
    own_ref[0] = owned(own_row, wet0, wet1)
    own_ref[1] = own_ref[0].T
    own_ref[2] = owned(down_row, down0, down1)
    own_ref[3] = owned(up_row, up0, up1)

    row_modes = [by_row_ref[p, pl.ds(local_own, rows), :] for p in range(ORDER)]
    up_modes = [by_row_ref[p, pl.ds(local_up, 1), :] for p in range(ORDER)]
    down_modes = [by_row_ref[p, pl.ds(local_down, 1), :] for p in range(ORDER)]

    def wide(v):
        return jnp.concatenate([v] * BLOCKS, axis=1)

    def group(c):
        return pl.ds(pl.multiple_of(c * BLOCKS, BLOCKS), BLOCKS)

    def line_of(ref, c, lane0=0):
        block = ref[group(c), lane0 : lane0 + LANES]
        return jnp.concatenate([block[t : t + 1, :] for t in range(BLOCKS)], axis=1)

    def cols(c, offset=0, extra=0):
        return pl.ds(pl.multiple_of(c * span + offset, LANES), span + extra)

    row_id = lax.broadcasted_iota(jnp.int32, (rows, span), 0)

    sub = lax.broadcasted_iota(jnp.int32, (8, LANES), 0)

    def sum_rows(parts):
        for bit in (4, 2, 1):
            lower = lax.rem(sub // bit, 2) == 0
            merged = []
            for t in range(bit):
                a, b = parts[t], parts[t + bit]
                other = jnp.where(lower, b, a)
                turned = pltpu.roll(other, 8 - bit, 0)
                if bit != 4:
                    turned = jnp.where(lower, turned, pltpu.roll(other, bit, 0))
                merged.append(jnp.where(lower, a, b) + turned)
            parts = merged
        return parts[0]

    def lift(c, field):
        for p in range(ORDER):
            parts = []
            for t in range(BLOCKS):
                block = field[:, t * LANES : (t + 1) * LANES] * row_modes[p]
                parts.append(functools.reduce(
                    lambda a, b: a + b, [block[i : i + 8] for i in range(0, rows, 8)]
                ))
            lift_ref[group(c), p * LANES : (p + 1) * LANES] = sum_rows(parts)

    half_row = lax.broadcasted_iota(jnp.int32, (LANES, ORDER * LANES), 0) < half
    half_col = (
        lax.rem(lax.broadcasted_iota(jnp.int32, (LANES, ORDER * LANES), 1), LANES) < half
    )
    same_half = half_row == half_col
    left8 = lax.broadcasted_iota(jnp.int32, (coarse // 2, LANES), 1) < half

    def packed_moments():
        sums = dot(own_ref[1], lift_ref[...])
        sums = jnp.where(same_half, sums, 0.0)
        g = dot(kron_ref[...], sums, ((1,), (1,)))
        g = g + pltpu.roll(g, half, 1)
        return jnp.where(left8, g[: coarse // 2], g[coarse // 2 :])

    def unpacked(packed):
        turned = pltpu.roll(packed, half, 1)
        return jnp.concatenate(
            [jnp.where(left8, packed, turned), jnp.where(left8, turned, packed)], axis=0
        )

    def remote(src, dst, send_sem, recv_sem, peer):
        return pltpu.make_async_remote_copy(
            src_ref=src, dst_ref=dst, send_sem=send_sem, recv_sem=recv_sem,
            device_id={"gy": peer}, device_id_type=MESH,
        )

    part = (8, 16, 8)
    first_row = (0, 0, 8)

    def exchange(k, peer_step):
        peer = lax.rem(me + peer_step, n)
        window = pl.ds(first_row[k], part[k])
        return remote(
            send_ref.at[k, window], recv_ref.at[k, me, window],
            all_send_sem.at[k, peer_step], all_recv_sem.at[k, me], peer,
        )

    def send_all(k):
        def go(step, carry):
            exchange(k, step).start()
            return carry

        lax.fori_loop(1, n, go, 0, unroll=n <= 16)
        recv_ref[k, me] = send_ref[k]

    def wait_all(k):
        window = pl.ds(first_row[k], part[k])

        def go(step, carry):
            peer = lax.rem(me + step, n)
            remote(
                send_ref.at[k, window], recv_ref.at[k, peer, window],
                all_send_sem.at[k, step], all_recv_sem.at[k, peer], peer,
            ).wait_recv()
            return carry

        lax.fori_loop(1, n, go, 0, unroll=n <= 16)
        parts = [recv_ref[k, i, first_row[k] : first_row[k] + part[k], :] for i in range(n)]
        while len(parts) > 1:
            parts = [parts[i] + parts[i + 1] for i in range(0, len(parts) - 1, 2)] + (
                [parts[-1]] if len(parts) % 2 else []
            )
        return parts[0]

    def row_up(src, dst, k):
        return remote(src, dst, row_send_sem.at[k], row_recv_sem.at[k], me + 1)

    def row_down(src, dst, k):
        return remote(src, dst, row_send_sem.at[k], row_recv_sem.at[k], me - 1)

    last = pl.ds(rows - 1, 1)
    first = pl.ds(0, 1)
    north_up = row_up(north_ref.at[last], nlo_ref, 0)
    sm_up = row_up(sm_ref.at[last], smlo_ref, 1)
    sm_down = row_down(sm_ref.at[first], smhi_ref, 2)
    q_up = row_up(q_ref.at[last], qlo_ref, 3)
    q_down = row_down(q_ref.at[first], qhi_ref, 4)

    @pl.when(jnp.logical_not(has_down))
    def _():
        for ref in (nlo_ref, smlo_ref, qlo_ref):
            ref[...] = jnp.zeros_like(ref)

    @pl.when(jnp.logical_not(has_up))
    def _():
        for ref in (smhi_ref, qhi_ref):
            ref[...] = jnp.zeros_like(ref)

    loads[0].wait()

    def first_moments(c, carry):
        lift(c, f_ref[:, cols(c)])
        return carry

    lax.fori_loop(0, chunks, first_moments, 0)
    send_ref[0, 0:8] = packed_moments()
    send_ref[0, 8:16] = jnp.zeros((8, LANES), jnp.float32)
    loads[1].wait()
    pl.semaphore_wait(barrier, n - 1)
    send_all(0)

    @pl.when(has_up)
    def _():
        north_up.start()

    loads[2].wait()
    loads[3].wait()
    loads[4].wait()
    loads[5].wait()

    identity = (
        lax.broadcasted_iota(jnp.int32, (coarse, coarse), 0)
        == lax.broadcasted_iota(jnp.int32, (coarse, coarse), 1)
    ).astype(jnp.float32)
    for k in range(coarse):
        block = inv_ref[:, k, :]
        ct_ref[k] = dot(identity, jnp.concatenate([block, block], axis=0), ((1,), (1,)))

    @pl.when(has_down)
    def _():
        north_up.wait_recv()

    def coefficients(c, energy):
        at = cols(c)
        here = line_of(mask_ref.at[0], c)
        raw = east_ref[:, pl.ds(pl.multiple_of(c * span, LANES), span + LANES)]
        e = raw[:, LANES:] * line_of(mask_ref.at[1], c)
        w = pltpu.roll(raw, 1, 1)[:, LANES:] * line_of(mask_ref.at[2], c)
        nf = north_ref[:, at] * jnp.where(row_id == rows - 1, line_of(mask_ref.at[3], c), here)
        sf = jnp.where(
            row_id == 0, nlo_ref[:, at] * line_of(mask_ref.at[4], c), pltpu.roll(nf, 1, 0)
        )
        center = (1.0 - here) + here * storage_ref[:, at] + e + w + nf + sf
        jacobi = 1.0 / center
        f = f_ref[:, at]
        smoothed = jacobi * f
        e_ref[:, at] = e
        w_ref[:, at] = w
        s_ref[:, at] = sf
        c_ref[:, at] = center
        j_ref[:, at] = jacobi
        sm_ref[:, at] = smoothed
        return energy + f * smoothed

    zero = jnp.zeros((rows, span), jnp.float32)

    energy_part = lax.fori_loop(0, chunks, coefficients, zero)

    @pl.when(has_up)
    def _():
        sm_up.start()

    @pl.when(has_down)
    def _():
        sm_down.start()

    def lane_sums(v):
        v = jnp.sum(v, axis=0, keepdims=True)
        return functools.reduce(
            lambda a, b: a + b, [v[:, t * LANES : (t + 1) * LANES] for t in range(BLOCKS)]
        )

    def dots_rows(a, b):
        r = lax.broadcasted_iota(jnp.int32, (8, LANES), 0)
        return jnp.where(r == 0, lane_sums(a), jnp.where(r == 1, lane_sums(b), 0.0))

    def total(block, row):
        return jnp.sum(block[row : row + 1, :], axis=1, keepdims=True)

    def expand(g):
        c = ct_ref[0] * g[0:1, :]
        for k in range(1, coarse):
            c = c + ct_ref[k] * g[k : k + 1, :]
        gc = jnp.sum(jnp.sum(g * c, axis=0, keepdims=True)[:, :half], axis=1, keepdims=True)
        d = dot(c.T, kron_ref[...])
        d = jnp.where(same_half, d, 0.0)
        spread_ref[...] = dot(own_ref[0], d)

        def edge(modes):
            return functools.reduce(
                lambda a, b: a + b,
                [modes[p] * d[:, p * LANES : (p + 1) * LANES] for p in range(ORDER)],
            )

        edge_ref[0] = dot(own_ref[2], edge(down_modes))
        edge_ref[1] = dot(own_ref[3], edge(up_modes))
        return gc

    def spread(c):
        return functools.reduce(
            lambda a, b: a + b,
            [wide(row_modes[p]) * line_of(spread_ref, c, p * LANES) for p in range(ORDER)],
        )

    def wrap(ref):
        ref[:, 0:LANES] = ref[:, width : width + LANES]
        ref[:, width + LANES : width + 2 * LANES] = ref[:, LANES : 2 * LANES]

    def operate(z_ref, c, low, high, nf):
        at = cols(c)
        window = z_ref[:, cols(c, 0, 2 * LANES)]
        size = span + 2 * LANES
        v = window[:, LANES : LANES + span]
        east_v = pltpu.roll(window, size - 1, 1)[:, LANES : LANES + span]
        west_v = pltpu.roll(window, 1, 1)[:, LANES : LANES + span]
        north_v = jnp.where(row_id == rows - 1, high, pltpu.roll(v, rows - 1, 0))
        south_v = jnp.where(row_id == 0, low, pltpu.roll(v, 1, 0))
        image = (
            c_ref[:, at] * v - e_ref[:, at] * east_v - w_ref[:, at] * west_v
            - nf * north_v - s_ref[:, at] * south_v
        )
        return v, image

    g = unpacked(wait_all(0))
    coarse_energy = expand(g)

    def north_of(c):
        return north_ref[:, cols(c)] * jnp.where(
            row_id == rows - 1, line_of(mask_ref.at[3], c), line_of(mask_ref.at[0], c)
        )

    def precondition0(c, carry):
        z0_ref[:, cols(c, LANES)] = sm_ref[:, cols(c)] + spread(c)
        return carry

    lax.fori_loop(0, chunks, precondition0, 0)
    wrap(z0_ref)

    @pl.when(has_down)
    def _():
        sm_up.wait_recv()

    @pl.when(has_up)
    def _():
        sm_down.wait_recv()

    def image0(c, along):
        at = cols(c)
        low = smlo_ref[:, at] + line_of(edge_ref.at[0], c)
        high = smhi_ref[:, at] + line_of(edge_ref.at[1], c)
        v, image = operate(z0_ref, c, low, high, north_of(c))
        im0_ref[:, at] = image
        q_ref[:, at] = j_ref[:, at] * image
        lift(c, image)
        return along + v * image

    along_part = lax.fori_loop(0, chunks, image0, zero)

    @pl.when(has_up)
    def _():
        q_up.start()

    @pl.when(has_down)
    def _():
        q_down.start()

    send_ref[1, 0:8] = packed_moments()
    send_ref[1, 8:16] = dots_rows(energy_part, along_part)
    send_all(1)
    sums = wait_all(1)
    energy = total(sums[8:16], 0) + coarse_energy
    alpha = energy / total(sums[8:16], 1)
    g = g - alpha * unpacked(sums[0:8])
    coarse_energy = expand(g)

    def precondition1(c, acc):
        at = cols(c)
        smoothed = sm_ref[:, at] - alpha * q_ref[:, at]
        residual = f_ref[:, at] - alpha * im0_ref[:, at]
        f_ref[:, at] = residual
        z1_ref[:, cols(c, LANES)] = smoothed + spread(c)
        return acc + residual * smoothed

    energy_part = lax.fori_loop(0, chunks, precondition1, zero)
    wrap(z1_ref)

    @pl.when(has_down)
    def _():
        q_up.wait_recv()

    @pl.when(has_up)
    def _():
        q_down.wait_recv()

    def image1(c, along):
        at = cols(c)
        low = smlo_ref[:, at] - alpha * qlo_ref[:, at] + line_of(edge_ref.at[0], c)
        high = smhi_ref[:, at] - alpha * qhi_ref[:, at] + line_of(edge_ref.at[1], c)
        v, image = operate(z1_ref, c, low, high, north_of(c))
        im1_ref[:, at] = image
        return along + v * image

    along_part = lax.fori_loop(0, chunks, image1, zero)
    send_ref[2, 0:8] = jnp.zeros((8, LANES), jnp.float32)
    send_ref[2, 8:16] = dots_rows(energy_part, along_part)
    send_all(2)
    sums = wait_all(2)
    energy_next = total(sums, 0) + coarse_energy
    beta = energy_next / energy
    alpha_next = energy_next / (total(sums, 1) - beta * energy_next / alpha)

    def finish(c, carry):
        at = cols(c)
        z0 = z0_ref[:, cols(c, LANES)]
        sol_ref[:, at] = alpha * z0 + alpha_next * (z1_ref[:, cols(c, LANES)] + beta * z0)
        res_ref[:, at] = f_ref[:, at] - alpha_next * (im1_ref[:, at] + beta * im0_ref[:, at])
        return carry

    lax.fori_loop(0, chunks, finish, 0)

    @pl.when(has_up)
    def _():
        north_up.wait_send()
        sm_up.wait_send()
        q_up.wait_send()

    @pl.when(has_down)
    def _():
        sm_down.wait_send()
        q_down.wait_send()

    for k in range(3):
        def drain(step, carry):
            exchange(k, step).wait_send()
            return carry

        lax.fori_loop(1, n, drain, 0, unroll=n <= 16)


def body(forcing, east, north, storage, coarse_inverse, membership, land):
    n = lax.axis_size("gy")
    rows, width = forcing.shape
    basins, coarse, _ = coarse_inverse.shape
    by_row, kron = tables()
    field = pltpu.VMEM((rows, width), jnp.float32)
    padded = pltpu.VMEM((rows, width + 2 * LANES), jnp.float32)
    line = pltpu.VMEM((1, width), jnp.float32)
    blocks = width // LANES
    hbm = pl.BlockSpec(memory_space=pl.ANY)
    vmem = pl.BlockSpec(memory_space=pltpu.VMEM)
    return pl.pallas_call(
        functools.partial(kernel, n),
        out_shape=[jax.ShapeDtypeStruct((rows, width), jnp.float32)] * 2,
        in_specs=[hbm] * 5 + [vmem] * 4,
        out_specs=[vmem] * 2,
        scratch_shapes=[
            field, padded, field, field, pltpu.VMEM((basins, coarse, coarse), jnp.float32),
            field, field, field, field, field, field, field, padded, padded, field, field,
            pltpu.VMEM((5, blocks, LANES), jnp.float32),
            pltpu.VMEM((4, blocks, LANES), jnp.float32),
            pltpu.VMEM((blocks, ORDER * LANES), jnp.float32),
            pltpu.VMEM((2, blocks, LANES), jnp.float32),
            pltpu.VMEM((blocks, ORDER * LANES), jnp.float32),
            pltpu.VMEM((coarse, coarse, LANES), jnp.float32),
            line, line, line, line, line,
            pltpu.VMEM((3, 16, LANES), jnp.float32),
            pltpu.VMEM((3, n, 16, LANES), jnp.float32),
            pltpu.SemaphoreType.DMA((6,)),
            pltpu.SemaphoreType.DMA((5,)),
            pltpu.SemaphoreType.DMA((5,)),
            pltpu.SemaphoreType.DMA((3, n)),
            pltpu.SemaphoreType.DMA((3, n)),
        ],
        compiler_params=pltpu.CompilerParams(
            collective_id=0, has_side_effects=True, vmem_limit_bytes=48 * 1024 * 1024
        ),
        name="solve",
    )(forcing, east, north, storage, coarse_inverse, membership, land, jnp.asarray(by_row), jnp.asarray(kron))


def solution(mesh):
    return jax.shard_map(
        body,
        mesh=mesh,
        in_specs=(
            P(("ens", "gy"), None),
            P("gy", None),
            P("gy", None),
            P("gy", None),
            P(),
            P(),
            P(),
        ),
        out_specs=(P(("ens", "gy"), None), P(("ens", "gy"), None)),
        check_vma=False,
    )
```

time: 180 us -> 40.2 us (0.22)
  blocking collectives: 96.3 us -> 0 us
  Pallas kernels: 0 us -> 32.3 us
  other arithmetic: 30.6 us -> 0 us
  local copies, waits for them, and re-layouts: 24.8 us -> 6.88 us
  starting transfers between devices: 11.4 us -> 0 us
  matrix products: 8.81 us -> 0 us
  between operations: 5.5 us -> 0.72 us
    psum x3 -> x0, blocking collectives: 96.3 us -> none  [reduce_coarse(): return lax.psum((partial_value, dots), 'gy')]
    pallas_call x0 -> x1, Pallas kernels: none -> 32.3 us  [body(): pl.pallas_call(functools.partial(kernel, n), out_shape=[jax.ShapeDtypeStr...]
    reduce_sum x9 -> x0, other arithmetic: 16.6 us -> none  [the longest x2 4.4 us: moments(): per_tile = jnp.sum(product, axis=2)]
    ppermute x5 -> x0, starting transfers between devices: 11.4 us -> none  [the longest x2 6.25 us: padded_2(): before = lax.ppermute(last, axis, up)]
    dot_general x9 -> x0, matrix products: 8.81 us -> none  [the longest x2 4.34 us: spread(): return wet * jnp.dot(row_modes.T, lifted, precision=HIGHEST)]
    mul x2 -> x0, local copies, waits for them, and re-layouts: 6.46 us -> none  [moments(): lifted[:, None, :] * col_modes[None, :, :]]
    slice x14 -> x0, local copies, waits for them, and re-layouts: 6.09 us -> none  [the longest x2 1.63 us: body(): above = wet_rows[1:]]
    another operation x2 -> x0, local copies, waits for them, and re-layouts: 6.05 us -> none  [spread(): per_col = jnp.repeat(per_tile.T, tile, axis=1).reshape(order, order, width)]
  transfers between devices with their start and end apart: 5 -> 0, of which waited for: 2 -> 0; matrix products, arithmetic and copies ran while one was open for 11% -> 0% of each run, Pallas kernels for 0% -> 0%
where the time goes in v1:
time: 40.2 us; the launch traced here: 39.9 us
  Pallas kernels  32.3 us (80%)
  local copies, waits for them, and re-layouts  6.88 us (17%)
  between operations  0.72 us (2%)
    pallas_call x1, Pallas kernels, body(): pl.pallas_call(functools.partial(kernel, n), out_shape=[jax.ShapeDtypeStr...  32.3 us
    unnamed x17, local copies, waits for them, and re-layouts  6.88 us

profile of v1, /device:TPU:0, one launch (start us, length us, event | category | flops | bytes accessed | tf_op | source)
XLA Modules:
  0.0 39.9 jit_solution(17611190150576119925)
XLA Ops:
  0.6 0.0 copy-start.3
  0.6 0.0 copy-start.4
  0.7 0.0 copy-start.6
  0.7 0.0 copy-start.5
  0.7 1.2 %copy.11.inverse_hbm = f32[64,16,16]{2,1,0:T(8,128)S(1)} copy(f32[64,16,16]{0,2,1:T(8,128)} %param.13) | data formatting | bytes 131072 | tf_op args[4]
  1.9 0.0 copy-done.3
  1.9 0.0 copy-done.4
  2.0 0.0 copy-done.6
  2.0 0.0 copy-done.5
  2.0 0.0 copy-start
  2.0 1.2 %copy-done = f32[16,16384]{1,0:T(8,128)S(1)} copy-done((f32[16,16384]{1,0:T(8,128)S(1)}, f32[16,16384]{1,0:T(8,128)}, u32[]{:S(2)}) %copy-start) | copy-done | bytes 1048600
  3.2 0.0 copy-start.1
  3.2 1.2 %copy-done.1 = f32[16,16384]{1,0:T(8,128)S(1)} copy-done((f32[16,16384]{1,0:T(8,128)S(1)}, f32[16,16384]{1,0:T(8,128)}, u32[]{:S(2)}) %copy-start.1) | copy-done | bytes 1048600
  4.4 0.0 copy-start.2
  4.4 1.2 %copy-done.2 = f32[16,16384]{1,0:T(8,128)S(1)} copy-done((f32[16,16384]{1,0:T(8,128)S(1)}, f32[16,16384]{1,0:T(8,128)}, u32[]{:S(2)}) %copy-start.2) | copy-done | bytes 1048600
  5.7 32.3 %solve.1 = (f32[16,16384]{1,0:T(8,128)S(1)}, f32[16,16384]{1,0:T(8,128)S(1)}) custom-call(f32[16,16384]{1,0:T(8,128)S(1)} %copy-done, f32[16,16384]{1,0:T(8,128)S(1)} %copy-done.1, f32[16,16384]{1,0:T(8,128)S(1)} %copy-done.2, f32[16,16384]{1,0:T(8,128)} %storage_hbm.1, f32[64,16,16]{2,1,0:T(8,128)S(1)} %copy.11.inverse_hbm, s32[4,256]{1,0:T(4,128)S(1)} %copy-done.5, ...), custom_call_target="tpu_custom_call" | custom-call | tf_op jit(solution)/shard_map/solve/pallas_call | solution.py:524
  38.0 1.0 %copy.14 = f32[16,16384]{1,0:T(8,128)} copy(f32[16,16384]{1,0:T(8,128)S(1)} %get-tuple-element.4) | data formatting | bytes 2097152
  39.0 1.0 %copy.15 = f32[16,16384]{1,0:T(8,128)} copy(f32[16,16384]{1,0:T(8,128)S(1)} %get-tuple-element.5) | data formatting | bytes 2097152
Async XLA Ops:
  0.6 1.3 %copy-start.3 = (f32[4,64,128]{2,1,0:T(8,128)S(1)}, f32[4,64,128]{2,1,0:T(8,128)}, u32[]{:S(2)}) copy-start(f32[4,64,128]{2,1,0:T(8,128)} %constant.4.clone.by_row_ref) | copy-start | bytes 393220
  0.6 1.3 %copy-start.4 = (f32[16,512]{1,0:T(8,128)S(1)}, f32[16,512]{1,0:T(8,128)}, u32[]{:S(2)}) copy-start(f32[16,512]{1,0:T(8,128)} %constant.5.clone.kron_ref) | copy-start | bytes 98308
  0.7 1.3 %copy-start.6 = (s32[4,256]{1,0:T(4,128)S(1)}, s32[4,256]{1,0:T(4,128)}, u32[]{:S(2)}) copy-start(s32[4,256]{1,0:T(4,128)} %land_ref.1) | copy-start | bytes 12292
  0.7 1.3 %copy-start.5 = (s32[4,256]{1,0:T(4,128)S(1)}, s32[4,256]{1,0:T(4,128)}, u32[]{:S(2)}) copy-start(s32[4,256]{1,0:T(4,128)} %membership_ref.1) | copy-start | bytes 12292
  2.0 1.2 %copy-start = (f32[16,16384]{1,0:T(8,128)S(1)}, f32[16,16384]{1,0:T(8,128)}, u32[]{:S(2)}) copy-start(f32[16,16384]{1,0:T(8,128)} %forcing_hbm.1) | copy-start | bytes 3145732
  3.2 1.2 %copy-start.1 = (f32[16,16384]{1,0:T(8,128)S(1)}, f32[16,16384]{1,0:T(8,128)}, u32[]{:S(2)}) copy-start(f32[16,16384]{1,0:T(8,128)} %east_hbm.1) | copy-start | bytes 3145732
  4.4 1.2 %copy-start.2 = (f32[16,16384]{1,0:T(8,128)S(1)}, f32[16,16384]{1,0:T(8,128)}, u32[]{:S(2)}) copy-start(f32[16,16384]{1,0:T(8,128)} %north_hbm.1) | copy-start | bytes 3145732

commit v2 on v1

--- a/solution.py
+++ b/solution.py
@@ -12,6 +12,8 @@
 ORDER = 4
 LANES = 128
 BLOCKS = 8
+VMEM = 67043328
+SPARE = 400 * 1024
 HIGHEST = lax.Precision.HIGHEST
 MESH = pl.DeviceIdType.MESH
 
@@ -36,10 +38,10 @@
 
 def kernel(
     n,
-    forcing_hbm, east_hbm, north_hbm, storage_hbm, inverse_hbm,
+    forcing_hbm, east_hbm, north_hbm, storage_hbm, inv_ref,
     membership_ref, land_ref, by_row_ref, kron_ref,
     sol_ref, res_ref,
-    f_ref, east_ref, north_ref, storage_ref, inv_ref,
+    f_ref, east_ref, north_ref, storage_ref,
     e_ref, w_ref, s_ref, c_ref, j_ref, sm_ref, q_ref, z0_ref, z1_ref, im0_ref, im1_ref,
     mask_ref, own_ref, spread_ref, edge_ref, lift_ref, ct_ref,
     nlo_ref, smlo_ref, smhi_ref, qlo_ref, qhi_ref,
@@ -47,8 +49,7 @@
     in_sem, row_send_sem, row_recv_sem, all_send_sem, all_recv_sem,
 ):
     rows, width = f_ref.shape
-    basins = inv_ref.shape[0]
-    coarse = inv_ref.shape[1]
+    coarse = inv_ref.shape[0]
     blocks = width // LANES
     half = LANES // 2
     span = BLOCKS * LANES
@@ -68,7 +69,6 @@
         load(east_hbm, east_ref.at[:, pl.ds(LANES, width)], 2),
         load(east_hbm.at[:, pl.ds(width - LANES, LANES)], east_ref.at[:, pl.ds(0, LANES)], 3),
         load(storage_hbm, storage_ref, 4),
-        load(inverse_hbm, inv_ref, 5),
     ]
     for copy in loads:
         copy.start()
@@ -289,15 +289,9 @@
     loads[2].wait()
     loads[3].wait()
     loads[4].wait()
-    loads[5].wait()
-
-    identity = (
-        lax.broadcasted_iota(jnp.int32, (coarse, coarse), 0)
-        == lax.broadcasted_iota(jnp.int32, (coarse, coarse), 1)
-    ).astype(jnp.float32)
+
     for k in range(coarse):
-        block = inv_ref[:, k, :]
-        ct_ref[k] = dot(identity, jnp.concatenate([block, block], axis=0), ((1,), (1,)))
+        ct_ref[k] = jnp.concatenate([inv_ref[k]] * 2, axis=1)
 
     @pl.when(has_down)
     def _():
@@ -514,20 +508,21 @@
     n = lax.axis_size("gy")
     rows, width = forcing.shape
     basins, coarse, _ = coarse_inverse.shape
+    inverse = jnp.transpose(coarse_inverse, (1, 2, 0))
     by_row, kron = tables()
     field = pltpu.VMEM((rows, width), jnp.float32)
     padded = pltpu.VMEM((rows, width + 2 * LANES), jnp.float32)
     line = pltpu.VMEM((1, width), jnp.float32)
     blocks = width // LANES
-    hbm = pl.BlockSpec(memory_space=pl.ANY)
+    hbm = pl.BlockSpec(memory_space=pltpu.HBM)
     vmem = pl.BlockSpec(memory_space=pltpu.VMEM)
     return pl.pallas_call(
         functools.partial(kernel, n),
         out_shape=[jax.ShapeDtypeStruct((rows, width), jnp.float32)] * 2,
-        in_specs=[hbm] * 5 + [vmem] * 4,
+        in_specs=[hbm] * 4 + [vmem] * 5,
         out_specs=[vmem] * 2,
         scratch_shapes=[
-            field, padded, field, field, pltpu.VMEM((basins, coarse, coarse), jnp.float32),
+            field, padded, field, field,
             field, field, field, field, field, field, field, padded, padded, field, field,
             pltpu.VMEM((5, blocks, LANES), jnp.float32),
             pltpu.VMEM((4, blocks, LANES), jnp.float32),
@@ -538,17 +533,17 @@
             line, line, line, line, line,
             pltpu.VMEM((3, 16, LANES), jnp.float32),
             pltpu.VMEM((3, n, 16, LANES), jnp.float32),
-            pltpu.SemaphoreType.DMA((6,)),
+            pltpu.SemaphoreType.DMA((5,)),
             pltpu.SemaphoreType.DMA((5,)),
             pltpu.SemaphoreType.DMA((5,)),
             pltpu.SemaphoreType.DMA((3, n)),
             pltpu.SemaphoreType.DMA((3, n)),
         ],
         compiler_params=pltpu.CompilerParams(
-            collective_id=0, has_side_effects=True, vmem_limit_bytes=48 * 1024 * 1024
+            collective_id=0, has_side_effects=True, vmem_limit_bytes=VMEM - 8 * rows * width - SPARE
         ),
         name="solve",
-    )(forcing, east, north, storage, coarse_inverse, membership, land, jnp.asarray(by_row), jnp.asarray(kron))
+    )(forcing, east, north, storage, inverse, membership, land, jnp.asarray(by_row), jnp.asarray(kron))
 
 
 def solution(mesh):

time: 40.2 us -> 38.6 us (0.960)
  local copies, waits for them, and re-layouts: 6.88 us -> 3.32 us
  Pallas kernels: 32.3 us -> 34.4 us
    unnamed x17 -> x4, local copies, waits for them, and re-layouts: 6.88 us -> 3.32 us
    pallas_call x1, Pallas kernels: 32.3 us -> 34.4 us  [body(): pl.pallas_call(functools.partial(kernel, n), out_shape=[jax.ShapeDtypeStr...]
where the time goes in v2:
time: 38.6 us; the launch traced here: 38.4 us
  Pallas kernels  34.4 us (89%)
  local copies, waits for them, and re-layouts  3.32 us (9%)
  between operations  0.65 us (2%)
    pallas_call x1, Pallas kernels, body(): pl.pallas_call(functools.partial(kernel, n), out_shape=[jax.ShapeDtypeStr...  34.4 us
    unnamed x4, local copies, waits for them, and re-layouts  3.32 us

profile of v2, /device:TPU:0, one launch (start us, length us, event | category | flops | bytes accessed | tf_op | source)
XLA Modules:
  0.0 38.4 jit_solution(1860633993056838180)
XLA Ops:
  0.6 34.4 %solve.1 = (f32[16,16384]{1,0:T(8,128)}, f32[16,16384]{1,0:T(8,128)}) custom-call(f32[16,16384]{1,0:T(8,128)} %forcing_hbm.1, f32[16,16384]{1,0:T(8,128)} %east_hbm.1, f32[16,16384]{1,0:T(8,128)} %north_hbm.1, f32[16,16384]{1,0:T(8,128)} %storage_hbm.1, f32[16,16,64]{2,1,0:T(8,128)} %bitcast.1, s32[4,256]{1,0:T(4,128)} %membership_ref.1, s32[4,256]{1,0:T(4,128)} %land_ref.1, ...), custom_call_target="tpu_custom_call" | custom-call | tf_op jit(solution)/shard_map/solve/pallas_call | solution.py:519
  35.1 0.0 copy-start
  35.1 2.4 %copy.13 = f32[16,16384]{1,0:T(8,128)} copy(f32[16,16384]{1,0:T(8,128)} %get-tuple-element.4) | data formatting | bytes 2097152
  37.4 0.0 copy-done
  37.4 1.0 %copy.14 = f32[16,16384]{1,0:T(8,128)} copy(f32[16,16384]{1,0:T(8,128)S(1)} %copy-done) | data formatting | bytes 2097152
Async XLA Ops:
  35.1 2.4 %copy-start = (f32[16,16384]{1,0:T(8,128)S(1)}, f32[16,16384]{1,0:T(8,128)}, u32[]{:S(2)}) copy-start(f32[16,16384]{1,0:T(8,128)} %get-tuple-element.5) | copy-start | bytes 3145732

commit v3 on v2

--- a/solution.py
+++ b/solution.py
@@ -12,9 +12,6 @@
 ORDER = 4
 LANES = 128
 BLOCKS = 8
-VMEM = 67043328
-SPARE = 400 * 1024
-HIGHEST = lax.Precision.HIGHEST
 MESH = pl.DeviceIdType.MESH
 
 
@@ -30,17 +27,32 @@
     return by_row, kron
 
 
+def halves(x):
+    high = x.astype(jnp.bfloat16)
+    return high, (x - high.astype(jnp.float32)).astype(jnp.bfloat16)
+
+
+def one_pass(a, b, contract):
+    return lax.dot_general(a, b, (contract, ((), ())), preferred_element_type=jnp.float32)
+
+
+def pick(a, b):
+    high, low = halves(b)
+    a = a.astype(jnp.bfloat16)
+    return one_pass(a, high, ((1,), (0,))) + one_pass(a, low, ((1,), (0,)))
+
+
 def dot(a, b, contract=((1,), (0,))):
-    return lax.dot_general(
-        a, b, (contract, ((), ())), precision=HIGHEST, preferred_element_type=jnp.float32
-    )
+    (ah, al), (bh, bl) = halves(a), halves(b)
+    return one_pass(ah, bh, contract) + (one_pass(ah, bl, contract) + one_pass(al, bh, contract))
 
 
 def kernel(
     n,
-    forcing_hbm, east_hbm, north_hbm, storage_hbm, inv_ref,
-    membership_ref, land_ref, by_row_ref, kron_ref,
+    forcing_hbm, east_hbm, north_hbm, storage_hbm, inv_hbm,
+    membership_hbm, land_hbm, by_row_hbm, kron_hbm,
     sol_ref, res_ref,
+    inv_ref, membership_ref, land_ref, by_row_ref, kron_ref,
     f_ref, east_ref, north_ref, storage_ref,
     e_ref, w_ref, s_ref, c_ref, j_ref, sm_ref, q_ref, z0_ref, z1_ref, im0_ref, im1_ref,
     mask_ref, own_ref, spread_ref, edge_ref, lift_ref, ct_ref,
@@ -63,6 +75,13 @@
     def load(src, dst, k):
         return pltpu.make_async_copy(src, dst, in_sem.at[k])
 
+    tables_in = [
+        load(membership_hbm, membership_ref, 5),
+        load(land_hbm, land_ref, 6),
+        load(by_row_hbm, by_row_ref, 7),
+        load(kron_hbm, kron_ref, 8),
+        load(inv_hbm, inv_ref, 9),
+    ]
     loads = [
         load(forcing_hbm, f_ref, 0),
         load(north_hbm, north_ref, 1),
@@ -70,7 +89,7 @@
         load(east_hbm.at[:, pl.ds(width - LANES, LANES)], east_ref.at[:, pl.ds(0, LANES)], 3),
         load(storage_hbm, storage_ref, 4),
     ]
-    for copy in loads:
+    for copy in tables_in + loads:
         copy.start()
 
     barrier = pltpu.get_barrier_semaphore()
@@ -82,6 +101,9 @@
         return carry
 
     lax.fori_loop(1, n, greet, 0)
+
+    for copy in tables_in:
+        copy.wait()
 
     own_row = start // TILE
     up_row = jnp.minimum((start + rows) // TILE, tile_rows - 1)
@@ -189,7 +211,7 @@
     left8 = lax.broadcasted_iota(jnp.int32, (coarse // 2, LANES), 1) < half
 
     def packed_moments():
-        sums = dot(own_ref[1], lift_ref[...])
+        sums = pick(own_ref[1], lift_ref[...])
         sums = jnp.where(same_half, sums, 0.0)
         g = dot(kron_ref[...], sums, ((1,), (1,)))
         g = g + pltpu.roll(g, half, 1)
@@ -207,7 +229,7 @@
             device_id={"gy": peer}, device_id_type=MESH,
         )
 
-    part = (8, 16, 8)
+    part = (8, 10, 2)
     first_row = (0, 0, 8)
 
     def exchange(k, peer_step):
@@ -219,12 +241,18 @@
         )
 
     def send_all(k):
-        def go(step, carry):
+        def go(i, carry):
+            step = n // 2 + (2 * (i % 2) - 1) * ((i + 1) // 2)
             exchange(k, step).start()
             return carry
 
-        lax.fori_loop(1, n, go, 0, unroll=n <= 16)
-        recv_ref[k, me] = send_ref[k]
+        if n <= 16:
+            for i in range(n - 1):
+                go(i, 0)
+        else:
+            lax.fori_loop(0, n - 1, go, 0)
+        window = pl.ds(first_row[k], part[k])
+        recv_ref[k, me, window] = send_ref[k, window]
 
     def wait_all(k):
         window = pl.ds(first_row[k], part[k])
@@ -277,7 +305,6 @@
 
     lax.fori_loop(0, chunks, first_moments, 0)
     send_ref[0, 0:8] = packed_moments()
-    send_ref[0, 8:16] = jnp.zeros((8, LANES), jnp.float32)
     loads[1].wait()
     pl.semaphore_wait(barrier, n - 1)
     send_all(0)
@@ -351,7 +378,7 @@
         gc = jnp.sum(jnp.sum(g * c, axis=0, keepdims=True)[:, :half], axis=1, keepdims=True)
         d = dot(c.T, kron_ref[...])
         d = jnp.where(same_half, d, 0.0)
-        spread_ref[...] = dot(own_ref[0], d)
+        spread_ref[...] = pick(own_ref[0], d)
 
         def edge(modes):
             return functools.reduce(
@@ -359,8 +386,8 @@
                 [modes[p] * d[:, p * LANES : (p + 1) * LANES] for p in range(ORDER)],
             )
 
-        edge_ref[0] = dot(own_ref[2], edge(down_modes))
-        edge_ref[1] = dot(own_ref[3], edge(up_modes))
+        edge_ref[0] = pick(own_ref[2], edge(down_modes))
+        edge_ref[1] = pick(own_ref[3], edge(up_modes))
         return gc
 
     def spread(c):
@@ -435,8 +462,8 @@
     send_ref[1, 8:16] = dots_rows(energy_part, along_part)
     send_all(1)
     sums = wait_all(1)
-    energy = total(sums[8:16], 0) + coarse_energy
-    alpha = energy / total(sums[8:16], 1)
+    energy = total(sums, 8) + coarse_energy
+    alpha = energy / total(sums, 9)
     g = g - alpha * unpacked(sums[0:8])
     coarse_energy = expand(g)
 
@@ -468,7 +495,6 @@
         return along + v * image
 
     along_part = lax.fori_loop(0, chunks, image1, zero)
-    send_ref[2, 0:8] = jnp.zeros((8, LANES), jnp.float32)
     send_ref[2, 8:16] = dots_rows(energy_part, along_part)
     send_all(2)
     sums = wait_all(2)
@@ -519,9 +545,14 @@
     return pl.pallas_call(
         functools.partial(kernel, n),
         out_shape=[jax.ShapeDtypeStruct((rows, width), jnp.float32)] * 2,
-        in_specs=[hbm] * 4 + [vmem] * 5,
+        in_specs=[hbm] * 9,
         out_specs=[vmem] * 2,
         scratch_shapes=[
+            pltpu.VMEM((coarse, coarse, basins), jnp.float32),
+            pltpu.VMEM(membership.shape, jnp.int32),
+            pltpu.VMEM(land.shape, jnp.int32),
+            pltpu.VMEM(by_row.shape, jnp.float32),
+            pltpu.VMEM(kron.shape, jnp.float32),
             field, padded, field, field,
             field, field, field, field, field, field, field, padded, padded, field, field,
             pltpu.VMEM((5, blocks, LANES), jnp.float32),
@@ -533,17 +564,23 @@
             line, line, line, line, line,
             pltpu.VMEM((3, 16, LANES), jnp.float32),
             pltpu.VMEM((3, n, 16, LANES), jnp.float32),
-            pltpu.SemaphoreType.DMA((5,)),
+            pltpu.SemaphoreType.DMA((10,)),
             pltpu.SemaphoreType.DMA((5,)),
             pltpu.SemaphoreType.DMA((5,)),
             pltpu.SemaphoreType.DMA((3, n)),
             pltpu.SemaphoreType.DMA((3, n)),
         ],
         compiler_params=pltpu.CompilerParams(
-            collective_id=0, has_side_effects=True, vmem_limit_bytes=VMEM - 8 * rows * width - SPARE
+            collective_id=0, has_side_effects=True, vmem_limit_bytes=48 * 1024 * 1024
         ),
         name="solve",
-    )(forcing, east, north, storage, inverse, membership, land, jnp.asarray(by_row), jnp.asarray(kron))
+    )(*(
+        pltpu.with_memory_space_constraint(x, pltpu.HBM)
+        for x in (
+            forcing, east, north, storage, inverse, membership, land,
+            jnp.asarray(by_row), jnp.asarray(kron),
+        )
+    ))
 
 
 def solution(mesh):

time: 38.6 us -> 33.9 us (0.88)
  Pallas kernels: 34.4 us -> 31.1 us
  local copies, waits for them, and re-layouts: 3.32 us -> 1.94 us
    pallas_call x1, Pallas kernels: 34.4 us -> 31.1 us  [body(): pl.pallas_call(functools.partial(kernel, n), out_shape=[jax.ShapeDtypeStr...]
    unnamed x4 -> x2, local copies, waits for them, and re-layouts: 3.32 us -> 1.94 us
where the time goes in v3:
time: 33.9 us; the launch traced here: 33.7 us
  Pallas kernels  31.1 us (92%)
  local copies, waits for them, and re-layouts  1.94 us (6%)
  between operations  0.64 us (2%)
    pallas_call x1, Pallas kernels, body(): pl.pallas_call(functools.partial(kernel, n), out_shape=[jax.ShapeDtypeStr...  31.1 us
    unnamed x2, local copies, waits for them, and re-layouts  1.94 us

profile of v3, /device:TPU:0, one launch (start us, length us, event | category | flops | bytes accessed | tf_op | source)
XLA Modules:
  0.0 33.7 jit_solution(416129973091911374)
XLA Ops:
  0.6 31.1 %solve.1 = (f32[16,16384]{1,0:T(8,128)S(1)}, f32[16,16384]{1,0:T(8,128)S(1)}) custom-call(f32[16,16384]{1,0:T(8,128)} %forcing_hbm.1, f32[16,16384]{1,0:T(8,128)} %east_hbm.1, f32[16,16384]{1,0:T(8,128)} %north_hbm.1, f32[16,16384]{1,0:T(8,128)} %storage_hbm.1, f32[16,16,64]{2,1,0:T(8,128)} %bitcast.1, s32[4,256]{1,0:T(4,128)} %membership_hbm.1, ...), custom_call_target="tpu_custom_call" | custom-call | tf_op jit(solution)/shard_map/solve/pallas_call | solution.py:545
  31.8 1.0 %copy.13 = f32[16,16384]{1,0:T(8,128)} copy(f32[16,16384]{1,0:T(8,128)S(1)} %get-tuple-element.4) | data formatting | bytes 2097152
  32.7 1.0 %copy.14 = f32[16,16384]{1,0:T(8,128)} copy(f32[16,16384]{1,0:T(8,128)S(1)} %get-tuple-element.5) | data formatting | bytes 2097152

commit v4 on v3

--- a/solution.py
+++ b/solution.py
@@ -54,7 +54,7 @@
     sol_ref, res_ref,
     inv_ref, membership_ref, land_ref, by_row_ref, kron_ref,
     f_ref, east_ref, north_ref, storage_ref,
-    e_ref, w_ref, s_ref, c_ref, j_ref, sm_ref, q_ref, z0_ref, z1_ref, im0_ref, im1_ref,
+    e_ref, w_ref, s_ref, c_ref, j_ref, sm_ref, q_ref, z0_ref, z1_ref, im0_ref, im1_ref, n_ref,
     mask_ref, own_ref, spread_ref, edge_ref, lift_ref, ct_ref,
     nlo_ref, smlo_ref, smhi_ref, qlo_ref, qhi_ref,
     send_ref, recv_ref,
@@ -142,22 +142,8 @@
 
     wet0, wet1 = wets(own_row)
     wet = jnp.where(left, wet0, wet1)
-    east_wet = jnp.where(
-        lane == half - 1, wet1, jnp.where(lane == LANES - 1, pltpu.roll(wet0, blocks - 1, 0), wet)
-    )
-    west_wet = jnp.where(lane == 0, pltpu.roll(wet1, 1, 0), jnp.where(lane == half, wet0, wet))
-    up0, up1 = wets(up_row)
-    down0, down1 = wets(down_row)
-    mask_ref[0] = wet
-    mask_ref[1] = wet * east_wet
-    mask_ref[2] = wet * west_wet
-    mask_ref[3] = jnp.where(has_up, wet * jnp.where(left, up0, up1), 0.0)
-    mask_ref[4] = jnp.where(has_down, wet * jnp.where(left, down0, down1), 0.0)
     own_ref[0] = owned(own_row, wet0, wet1)
     own_ref[1] = own_ref[0].T
-    own_ref[2] = owned(down_row, down0, down1)
-    own_ref[3] = owned(up_row, up0, up1)
-
     row_modes = [by_row_ref[p, pl.ds(local_own, rows), :] for p in range(ORDER)]
     up_modes = [by_row_ref[p, pl.ds(local_up, 1), :] for p in range(ORDER)]
     down_modes = [by_row_ref[p, pl.ds(local_down, 1), :] for p in range(ORDER)]
@@ -273,6 +259,13 @@
             )
         return parts[0]
 
+    def drain(k):
+        def go(step, carry):
+            exchange(k, step).wait_send()
+            return carry
+
+        lax.fori_loop(1, n, go, 0, unroll=n <= 16)
+
     def row_up(src, dst, k):
         return remote(src, dst, row_send_sem.at[k], row_recv_sem.at[k], me + 1)
 
@@ -313,6 +306,20 @@
     def _():
         north_up.start()
 
+    east_wet = jnp.where(
+        lane == half - 1, wet1, jnp.where(lane == LANES - 1, pltpu.roll(wet0, blocks - 1, 0), wet)
+    )
+    west_wet = jnp.where(lane == 0, pltpu.roll(wet1, 1, 0), jnp.where(lane == half, wet0, wet))
+    up0, up1 = wets(up_row)
+    down0, down1 = wets(down_row)
+    mask_ref[0] = wet
+    mask_ref[1] = wet * east_wet
+    mask_ref[2] = wet * west_wet
+    mask_ref[3] = jnp.where(has_up, wet * jnp.where(left, up0, up1), 0.0)
+    mask_ref[4] = jnp.where(has_down, wet * jnp.where(left, down0, down1), 0.0)
+    own_ref[2] = owned(down_row, down0, down1)
+    own_ref[3] = owned(up_row, up0, up1)
+
     loads[2].wait()
     loads[3].wait()
     loads[4].wait()
@@ -323,6 +330,18 @@
     @pl.when(has_down)
     def _():
         north_up.wait_recv()
+
+    zero = jnp.zeros((8, LANES), jnp.float32)
+
+    def fold(v):
+        parts = [
+            v[i : i + 8, t * LANES : (t + 1) * LANES]
+            for i in range(0, rows, 8)
+            for t in range(BLOCKS)
+        ]
+        while len(parts) > 1:
+            parts = [parts[i] + parts[i + 1] for i in range(0, len(parts), 2)]
+        return parts[0]
 
     def coefficients(c, energy):
         at = cols(c)
@@ -341,12 +360,11 @@
         e_ref[:, at] = e
         w_ref[:, at] = w
         s_ref[:, at] = sf
+        n_ref[:, at] = nf
         c_ref[:, at] = center
         j_ref[:, at] = jacobi
         sm_ref[:, at] = smoothed
-        return energy + f * smoothed
-
-    zero = jnp.zeros((rows, span), jnp.float32)
+        return energy + fold(f * smoothed)
 
     energy_part = lax.fori_loop(0, chunks, coefficients, zero)
 
@@ -359,10 +377,7 @@
         sm_down.start()
 
     def lane_sums(v):
-        v = jnp.sum(v, axis=0, keepdims=True)
-        return functools.reduce(
-            lambda a, b: a + b, [v[:, t * LANES : (t + 1) * LANES] for t in range(BLOCKS)]
-        )
+        return jnp.sum(v, axis=0, keepdims=True)
 
     def dots_rows(a, b):
         r = lax.broadcasted_iota(jnp.int32, (8, LANES), 0)
@@ -400,7 +415,7 @@
         ref[:, 0:LANES] = ref[:, width : width + LANES]
         ref[:, width + LANES : width + 2 * LANES] = ref[:, LANES : 2 * LANES]
 
-    def operate(z_ref, c, low, high, nf):
+    def operate(z_ref, c, low, high):
         at = cols(c)
         window = z_ref[:, cols(c, 0, 2 * LANES)]
         size = span + 2 * LANES
@@ -411,17 +426,12 @@
         south_v = jnp.where(row_id == 0, low, pltpu.roll(v, 1, 0))
         image = (
             c_ref[:, at] * v - e_ref[:, at] * east_v - w_ref[:, at] * west_v
-            - nf * north_v - s_ref[:, at] * south_v
+            - n_ref[:, at] * north_v - s_ref[:, at] * south_v
         )
         return v, image
 
     g = unpacked(wait_all(0))
     coarse_energy = expand(g)
-
-    def north_of(c):
-        return north_ref[:, cols(c)] * jnp.where(
-            row_id == rows - 1, line_of(mask_ref.at[3], c), line_of(mask_ref.at[0], c)
-        )
 
     def precondition0(c, carry):
         z0_ref[:, cols(c, LANES)] = sm_ref[:, cols(c)] + spread(c)
@@ -442,11 +452,11 @@
         at = cols(c)
         low = smlo_ref[:, at] + line_of(edge_ref.at[0], c)
         high = smhi_ref[:, at] + line_of(edge_ref.at[1], c)
-        v, image = operate(z0_ref, c, low, high, north_of(c))
+        v, image = operate(z0_ref, c, low, high)
         im0_ref[:, at] = image
         q_ref[:, at] = j_ref[:, at] * image
         lift(c, image)
-        return along + v * image
+        return along + fold(v * image)
 
     along_part = lax.fori_loop(0, chunks, image0, zero)
 
@@ -461,6 +471,7 @@
     send_ref[1, 0:8] = packed_moments()
     send_ref[1, 8:16] = dots_rows(energy_part, along_part)
     send_all(1)
+    drain(0)
     sums = wait_all(1)
     energy = total(sums, 8) + coarse_energy
     alpha = energy / total(sums, 9)
@@ -473,7 +484,7 @@
         residual = f_ref[:, at] - alpha * im0_ref[:, at]
         f_ref[:, at] = residual
         z1_ref[:, cols(c, LANES)] = smoothed + spread(c)
-        return acc + residual * smoothed
+        return acc + fold(residual * smoothed)
 
     energy_part = lax.fori_loop(0, chunks, precondition1, zero)
     wrap(z1_ref)
@@ -490,13 +501,14 @@
         at = cols(c)
         low = smlo_ref[:, at] - alpha * qlo_ref[:, at] + line_of(edge_ref.at[0], c)
         high = smhi_ref[:, at] - alpha * qhi_ref[:, at] + line_of(edge_ref.at[1], c)
-        v, image = operate(z1_ref, c, low, high, north_of(c))
+        v, image = operate(z1_ref, c, low, high)
         im1_ref[:, at] = image
-        return along + v * image
+        return along + fold(v * image)
 
     along_part = lax.fori_loop(0, chunks, image1, zero)
     send_ref[2, 8:16] = dots_rows(energy_part, along_part)
     send_all(2)
+    drain(1)
     sums = wait_all(2)
     energy_next = total(sums, 0) + coarse_energy
     beta = energy_next / energy
@@ -522,12 +534,7 @@
         sm_down.wait_send()
         q_down.wait_send()
 
-    for k in range(3):
-        def drain(step, carry):
-            exchange(k, step).wait_send()
-            return carry
-
-        lax.fori_loop(1, n, drain, 0, unroll=n <= 16)
+    drain(2)
 
 
 def body(forcing, east, north, storage, coarse_inverse, membership, land):
@@ -554,7 +561,7 @@
             pltpu.VMEM(by_row.shape, jnp.float32),
             pltpu.VMEM(kron.shape, jnp.float32),
             field, padded, field, field,
-            field, field, field, field, field, field, field, padded, padded, field, field,
+            field, field, field, field, field, field, field, padded, padded, field, field, field,
             pltpu.VMEM((5, blocks, LANES), jnp.float32),
             pltpu.VMEM((4, blocks, LANES), jnp.float32),
             pltpu.VMEM((blocks, ORDER * LANES), jnp.float32),

time: 33.9 us -> 33.9 us (level)
  no operation moved by 1% of the time
where the time goes in v4:
time: 33.9 us; the launch traced here: 33.7 us
  Pallas kernels  31.1 us (92%)
  local copies, waits for them, and re-layouts  1.94 us (6%)
  between operations  0.64 us (2%)
    pallas_call x1, Pallas kernels, body(): pl.pallas_call(functools.partial(kernel, n), out_shape=[jax.ShapeDtypeStr...  31.1 us
    unnamed x2, local copies, waits for them, and re-layouts  1.94 us

profile of v4, /device:TPU:0, one launch (start us, length us, event | category | flops | bytes accessed | tf_op | source)
XLA Modules:
  0.0 33.7 jit_solution(13725022770484404297)
XLA Ops:
  0.6 31.1 %solve.1 = (f32[16,16384]{1,0:T(8,128)S(1)}, f32[16,16384]{1,0:T(8,128)S(1)}) custom-call(f32[16,16384]{1,0:T(8,128)} %forcing_hbm.1, f32[16,16384]{1,0:T(8,128)} %east_hbm.1, f32[16,16384]{1,0:T(8,128)} %north_hbm.1, f32[16,16384]{1,0:T(8,128)} %storage_hbm.1, f32[16,16,64]{2,1,0:T(8,128)} %bitcast.1, s32[4,256]{1,0:T(4,128)} %membership_hbm.1, ...), custom_call_target="tpu_custom_call" | custom-call | tf_op jit(solution)/shard_map/solve/pallas_call | solution.py:552
  31.8 1.0 %copy.13 = f32[16,16384]{1,0:T(8,128)} copy(f32[16,16384]{1,0:T(8,128)S(1)} %get-tuple-element.4) | data formatting | bytes 2097152
  32.8 1.0 %copy.14 = f32[16,16384]{1,0:T(8,128)} copy(f32[16,16384]{1,0:T(8,128)S(1)} %get-tuple-element.5) | data formatting | bytes 2097152

commit v5 on v4

--- a/solution.py
+++ b/solution.py
@@ -300,11 +300,12 @@
     send_ref[0, 0:8] = packed_moments()
     loads[1].wait()
     pl.semaphore_wait(barrier, n - 1)
+
+    @pl.when(has_up)
+    def _():
+        north_up.start()
+
     send_all(0)
-
-    @pl.when(has_up)
-    def _():
-        north_up.start()
 
     east_wet = jnp.where(
         lane == half - 1, wet1, jnp.where(lane == LANES - 1, pltpu.roll(wet0, blocks - 1, 0), wet)
@@ -327,16 +328,13 @@
     for k in range(coarse):
         ct_ref[k] = jnp.concatenate([inv_ref[k]] * 2, axis=1)
 
-    @pl.when(has_down)
-    def _():
-        north_up.wait_recv()
 
     zero = jnp.zeros((8, LANES), jnp.float32)
 
     def fold(v):
         parts = [
             v[i : i + 8, t * LANES : (t + 1) * LANES]
-            for i in range(0, rows, 8)
+            for i in range(0, v.shape[0], 8)
             for t in range(BLOCKS)
         ]
         while len(parts) > 1:
@@ -350,9 +348,7 @@
         e = raw[:, LANES:] * line_of(mask_ref.at[1], c)
         w = pltpu.roll(raw, 1, 1)[:, LANES:] * line_of(mask_ref.at[2], c)
         nf = north_ref[:, at] * jnp.where(row_id == rows - 1, line_of(mask_ref.at[3], c), here)
-        sf = jnp.where(
-            row_id == 0, nlo_ref[:, at] * line_of(mask_ref.at[4], c), pltpu.roll(nf, 1, 0)
-        )
+        sf = jnp.where(row_id == 0, 0.0, pltpu.roll(nf, 1, 0))
         center = (1.0 - here) + here * storage_ref[:, at] + e + w + nf + sf
         jacobi = 1.0 / center
         f = f_ref[:, at]
@@ -364,13 +360,34 @@
         c_ref[:, at] = center
         j_ref[:, at] = jacobi
         sm_ref[:, at] = smoothed
-        return energy + fold(f * smoothed)
+        return energy + fold(jnp.where(row_id == 0, 0.0, f * smoothed))
 
     energy_part = lax.fori_loop(0, chunks, coefficients, zero)
 
     @pl.when(has_up)
     def _():
         sm_up.start()
+
+    @pl.when(has_down)
+    def _():
+        north_up.wait_recv()
+
+    row8 = lax.broadcasted_iota(jnp.int32, (8, span), 0)
+
+    def first_row_of(c, energy):
+        at = cols(c)
+        south = jnp.where(row8 == 0, nlo_ref[:, at] * line_of(mask_ref.at[4], c), 0.0)
+        s_ref[0:8, at] = s_ref[0:8, at] + south
+        center = c_ref[0:8, at] + south
+        jacobi = 1.0 / center
+        f = f_ref[0:8, at]
+        smoothed = jacobi * f
+        c_ref[0:8, at] = center
+        j_ref[0:8, at] = jacobi
+        sm_ref[0:8, at] = smoothed
+        return energy + fold(jnp.where(row8 == 0, f * smoothed, 0.0))
+
+    energy_part = lax.fori_loop(0, chunks, first_row_of, energy_part)
 
     @pl.when(has_down)
     def _():

time: 33.9 us -> 32.7 us (0.965)
  Pallas kernels: 31.1 us -> 29.9 us
    pallas_call x1, Pallas kernels: 31.1 us -> 29.9 us  [body(): pl.pallas_call(functools.partial(kernel, n), out_shape=[jax.ShapeDtypeStr...]
where the time goes in v5:
time: 32.7 us; the launch traced here: 32.5 us
  Pallas kernels  29.9 us (91%)
  local copies, waits for them, and re-layouts  1.94 us (6%)
  between operations  0.64 us (2%)
    pallas_call x1, Pallas kernels, body(): pl.pallas_call(functools.partial(kernel, n), out_shape=[jax.ShapeDtypeStr...  29.9 us
    unnamed x2, local copies, waits for them, and re-layouts  1.94 us

profile of v5, /device:TPU:0, one launch (start us, length us, event | category | flops | bytes accessed | tf_op | source)
XLA Modules:
  0.0 32.5 jit_solution(16921722019674865272)
XLA Ops:
  0.6 29.9 %solve.1 = (f32[16,16384]{1,0:T(8,128)S(1)}, f32[16,16384]{1,0:T(8,128)S(1)}) custom-call(f32[16,16384]{1,0:T(8,128)} %forcing_hbm.1, f32[16,16384]{1,0:T(8,128)} %east_hbm.1, f32[16,16384]{1,0:T(8,128)} %north_hbm.1, f32[16,16384]{1,0:T(8,128)} %storage_hbm.1, f32[16,16,64]{2,1,0:T(8,128)} %bitcast.1, s32[4,256]{1,0:T(4,128)} %membership_hbm.1, ...), custom_call_target="tpu_custom_call" | custom-call | tf_op jit(solution)/shard_map/solve/pallas_call | solution.py:569
  30.5 1.0 %copy.13 = f32[16,16384]{1,0:T(8,128)} copy(f32[16,16384]{1,0:T(8,128)S(1)} %get-tuple-element.4) | data formatting | bytes 2097152
  31.5 1.0 %copy.14 = f32[16,16384]{1,0:T(8,128)} copy(f32[16,16384]{1,0:T(8,128)S(1)} %get-tuple-element.5) | data formatting | bytes 2097152

commit v6 on v5

--- a/solution.py
+++ b/solution.py
@@ -100,7 +100,7 @@
         )
         return carry
 
-    lax.fori_loop(1, n, greet, 0)
+    lax.fori_loop(1, n, greet, 0, unroll=n <= 16)
 
     for copy in tables_in:
         copy.wait()
@@ -526,6 +526,18 @@
     send_ref[2, 8:16] = dots_rows(energy_part, along_part)
     send_all(2)
     drain(1)
+    @pl.when(has_up)
+    def _():
+        north_up.wait_send()
+        sm_up.wait_send()
+        q_up.wait_send()
+
+    @pl.when(has_down)
+    def _():
+        sm_down.wait_send()
+        q_down.wait_send()
+
+    drain(2)
     sums = wait_all(2)
     energy_next = total(sums, 0) + coarse_energy
     beta = energy_next / energy
@@ -539,19 +551,6 @@
         return carry
 
     lax.fori_loop(0, chunks, finish, 0)
-
-    @pl.when(has_up)
-    def _():
-        north_up.wait_send()
-        sm_up.wait_send()
-        q_up.wait_send()
-
-    @pl.when(has_down)
-    def _():
-        sm_down.wait_send()
-        q_down.wait_send()
-
-    drain(2)
 
 
 def body(forcing, east, north, storage, coarse_inverse, membership, land):

time: 32.7 us -> 32.6 us (level)
  no operation moved by 1% of the time
where the time goes in v6:
time: 32.6 us; the launch traced here: 32.5 us
  Pallas kernels  29.9 us (92%)
  local copies, waits for them, and re-layouts  1.94 us (6%)
  between operations  0.64 us (2%)
    pallas_call x1, Pallas kernels, body(): pl.pallas_call(functools.partial(kernel, n), out_shape=[jax.ShapeDtypeStr...  29.9 us
    unnamed x2, local copies, waits for them, and re-layouts  1.94 us

profile of v6, /device:TPU:0, one launch (start us, length us, event | category | flops | bytes accessed | tf_op | source)
XLA Modules:
  0.0 32.5 jit_solution(5902109835510913862)
XLA Ops:
  0.6 29.9 %solve.1 = (f32[16,16384]{1,0:T(8,128)S(1)}, f32[16,16384]{1,0:T(8,128)S(1)}) custom-call(f32[16,16384]{1,0:T(8,128)} %forcing_hbm.1, f32[16,16384]{1,0:T(8,128)} %east_hbm.1, f32[16,16384]{1,0:T(8,128)} %north_hbm.1, f32[16,16384]{1,0:T(8,128)} %storage_hbm.1, f32[16,16,64]{2,1,0:T(8,128)} %bitcast.1, s32[4,256]{1,0:T(4,128)} %membership_hbm.1, ...), custom_call_target="tpu_custom_call" | custom-call | tf_op jit(solution)/shard_map/solve/pallas_call | solution.py:568
  30.5 1.0 %copy.13 = f32[16,16384]{1,0:T(8,128)} copy(f32[16,16384]{1,0:T(8,128)S(1)} %get-tuple-element.4) | data formatting | bytes 2097152
  31.5 1.0 %copy.14 = f32[16,16384]{1,0:T(8,128)} copy(f32[16,16384]{1,0:T(8,128)S(1)} %get-tuple-element.5) | data formatting | bytes 2097152
